TPU v7x, 32 devices: a whole 2x2x4 slice. The times are simulated.
32 devices in a mesh: energy: 2 (over y), slab: 16 (over z, x, core).
Axes of the slice: x: 2, y: 2, z: 4, core: 2. Of those that a mesh axis runs over, the one named last changes fastest.
Arguments:
- slab_green: bfloat16 [2, 128, 128, 128], P(None, ('energy', 'slab')), parts along dimension 1, may hold values from -1 to 1, as said below
- coupling: bfloat16 [2, 128, 128, 128], P(None, ('energy', 'slab')), parts along dimension 1, may hold values from -40 to 40
- left_lead_surface: bfloat16 [4, 128, 128], P('energy'), parts along dimension 0, may hold values from -8 to 8, as said below
- sigma_right: bfloat16 [4, 128, 128], P('energy'), parts along dimension 0, may hold values from -120 to 120, as said below
Outputs:
- green_diagonal: float32 [2, 128, 128, 128], P(None, ('energy', 'slab')), parts along dimension 1
There are 2 independent parts, one for each index of `energy`. A program takes and returns all parts, laid end to end along the dimension named above; each array names one. Nothing has to cross between parts.
Inputs may be any that keep to these rules, and one draw needn't show every extreme that they name: Each block of slab_green, both parts, equals its own transpose. `left_lead_surface`: both parts equal their own transposes. `sigma_right`: both parts equal their own transposes.
All inputs are finite; a program needn't handle non-finite values.
Results may differ from a plain program's by a relative error of at most 0.035.
Values may be sent and summed in bfloat16 or wider, within the bound.
A program may use at most 128 MiB of HBM per device.

v0:
```python
import functools

import jax
import jax.numpy as jnp
from jax import lax
from jax.experimental import pallas as pl
from jax.experimental.pallas import tpu as pltpu
from jax.sharding import PartitionSpec as P

MESH = pl.DeviceIdType.MESH
BF = jnp.bfloat16
F32 = jnp.float32


def wide(value):
    return jnp.concatenate([value[0], value[1]], axis=1)


def halves(out):
    width = out.shape[1] // 2
    return out[:, :width], out[:, width:]


def low(value):
    return value[0].astype(BF), value[1].astype(BF)


def plus(a, b):
    return a[0] + b[0], a[1] + b[1]


def times(rows, right):
    weights = jnp.concatenate(
        [wide(right), jnp.concatenate([-right[1], right[0]], axis=1)], axis=0
    )
    return jnp.dot(rows, weights, preferred_element_type=F32)


def times_transpose(rows, right):
    weights = jnp.concatenate(
        [
            jnp.concatenate([right[0], -right[1]], axis=1),
            jnp.concatenate([right[1], right[0]], axis=1),
        ],
        axis=0,
    )
    return lax.dot_general(rows, weights, (((1,), (1,)), ((), ())), preferred_element_type=F32)


def product(a, b):
    return low(halves(times(wide(a), b)))


def sandwich(factor, middle):
    inner = times(wide(factor), low(middle)).astype(BF)
    return halves(times_transpose(inner, factor))


def get(ref, *index):
    return ref[(*index, 0)], ref[(*index, 1)]


def put(ref, value, *index):
    ref[(*index, 0)] = value[0].astype(ref.dtype)
    ref[(*index, 1)] = value[1].astype(ref.dtype)


def kernel(
    rounds,
    green,
    link,
    lead,
    sigma,
    out,
    own,
    pair,
    board,
    factors,
    base,
    enter,
    onward,
    ends,
    send_sem,
    recv_sem,
):
    layers, width = green.shape[1], green.shape[2]
    energy, me = lax.axis_index("energy"), lax.axis_index("slab")
    role, chip = me % 2, me // 2
    mate = me + 1 - 2 * role
    bits = [(chip // 2**r) % 2 for r in range(rounds)]
    peers = [me + (1 - 2 * bits[r]) * 2 ** (r + 1) for r in range(rounds)]
    sides = [(bits[r] + role) % 2 for r in range(rounds)]

    barrier = pltpu.get_barrier_semaphore()
    for other in [mate] + peers:
        pl.semaphore_signal(barrier, inc=1, device_id=(energy, other), device_id_type=MESH)
    pl.semaphore_wait(barrier, rounds + 1)

    def remote(source, target, other, k):
        return pltpu.make_async_remote_copy(
            src_ref=source,
            dst_ref=target,
            send_sem=send_sem.at[k],
            recv_sem=recv_sem.at[k],
            device_id=(energy, other),
            device_id_type=MESH,
        )

    g = [(green[0, i], green[1, i]) for i in range(layers)]
    c = [(link[0, i], link[1, i]) for i in range(layers)]
    ahead = [low(halves(times_transpose(wide(g[i]), c[i]))) for i in range(layers)]
    back = [product(c[i], g[i]) for i in range(layers)]
    hop = [halves(times_transpose(wide(back[i]), c[i])) for i in range(layers)]

    m_up, s_up = [ahead[0]], [g[0]]
    m_down, s_down = [back[-1]], [hop[-1]]
    for i in range(1, layers):
        s_up.append(plus(sandwich(ahead[i], s_up[-1]), g[i]))
        m_up.append(product(ahead[i], m_up[-1]))
        j = layers - 1 - i
        s_down.insert(0, plus(sandwich(back[j], s_down[0]), hop[j]))
        m_down.insert(0, product(back[j], m_down[0]))

    put(own, m_up[-1], role, 0)
    put(own, s_up[-1], role, 1)
    put(own, m_down[0], 1 - role, 0)
    put(own, s_down[0], 1 - role, 1)
    copy = remote(own.at[1], pair, mate, 0)
    copy.start()

    for i in range(layers):
        put(factors, m_up[i], role, i)
        if i + 1 < layers:
            put(factors, product(g[i], m_down[i + 1]), 1 - role, i)
            put(base, plus(s_up[i], sandwich(g[i], s_down[i + 1])), i)
        else:
            put(factors, g[i], 1 - role, i)
            put(base, s_up[i], i)

    copy.wait()

    def merged(m_first, s_first, m_second, s_second):
        return (
            product(m_second, m_first),
            plus(sandwich(m_second, s_first), s_second),
        )

    total = merged(get(own, 0, 0), get(own, 0, 1), get(pair, 0), get(pair, 1))
    forward = role == 0
    start = (
        jnp.where(forward, lead[0], sigma[0]),
        jnp.where(forward, lead[1], sigma[1]),
    )
    row = lax.broadcasted_iota(jnp.int32, (width, width), 0)
    column = lax.broadcasted_iota(jnp.int32, (width, width), 1)
    square = jnp.where(row == column, 1.0, 0.0).astype(F32)
    nothing = jnp.zeros((width, width), F32)
    m_before, s_before = (square.astype(BF), nothing.astype(BF)), (nothing, nothing)

    def pick(side, a, b):
        return jnp.where(side == 1, a[0], b[0]), jnp.where(side == 1, a[1], b[1])

    pending = None
    for r in range(rounds - 1):
        put(board, total[0], r, sides[r], 0)
        put(board, total[1], r, sides[r], 1)
        copy = remote(board.at[r, sides[r]], board.at[r, sides[r]], peers[r], 1 + r)
        copy.start()
        if pending is not None:
            m_before, s_before = pending()
        copy.wait()
        first, second = (get(board, r, 0, 0), get(board, r, 0, 1)), (get(board, r, 1, 0), get(board, r, 1, 1))
        total = merged(*first, *second)

        def pending(r=r, first=first, m_old=m_before, s_old=s_before):
            if r == 0:
                return (
                    pick(sides[0], first[0], m_old),
                    pick(sides[0], (first[1][0].astype(F32), first[1][1].astype(F32)), s_old),
                )
            m_new, s_new = merged(*first, m_old, s_old)
            return pick(sides[r], m_new, m_old), pick(sides[r], s_new, s_old)

    last = rounds - 1
    put(onward, plus(sandwich(total[0], start), total[1]))
    copy = remote(onward, enter, peers[last], rounds)

    @pl.when(sides[last] == 0)
    def _():
        copy.start()
        put(enter, start)

    if pending is not None:
        m_before, s_before = pending()

    @pl.when(sides[last] == 1)
    def _():
        copy.wait_recv()

    entering = plus(sandwich(m_before, get(enter)), s_before)
    put(ends, entering, role)
    put(pair, plus(sandwich(get(own, 0, 0), entering), get(own, 0, 1)), 0)
    share = remote(pair.at[0], ends.at[role], mate, rounds + 1)
    share.start()

    def spread(k, middle):
        rows = jnp.concatenate([wide(get(factors, k, i)) for i in range(layers)], axis=0)
        inner = times(rows, low(middle)).astype(BF)
        return [
            halves(times_transpose(inner[i * width : (i + 1) * width], get(factors, k, i)))
            for i in range(layers)
        ]

    mine = spread(0, entering)
    for i in range(layers):
        put(base, plus(get(base, i), mine[i]), i)
    share.wait()
    theirs = spread(1, get(ends, 1 - role))
    for i in range(layers):
        value = plus(get(base, i), theirs[i])
        out[0, i] = value[0]
        out[1, i] = value[1]

    @pl.when(sides[last] == 0)
    def _():
        copy.wait_send()


def solution(mesh):
    peers = mesh.shape["slab"]
    rounds = (peers // 2).bit_length() - 1

    def local(slab_green, coupling, left_lead_surface, sigma_right):
        layers, width = slab_green.shape[1], slab_green.shape[2]
        vmem = pl.BlockSpec(memory_space=pltpu.VMEM)
        block = (2, width, width)
        return pl.pallas_call(
            functools.partial(kernel, rounds),
            out_shape=jax.ShapeDtypeStruct(slab_green.shape, F32),
            in_specs=[vmem] * 4,
            out_specs=vmem,
            scratch_shapes=[
                pltpu.VMEM((2, 2, *block), BF),
                pltpu.VMEM((2, *block), BF),
                pltpu.VMEM((max(rounds - 1, 1), 2, 2, *block), BF),
                pltpu.VMEM((2, layers, *block), BF),
                pltpu.VMEM((layers, *block), F32),
                pltpu.VMEM(block, BF),
                pltpu.VMEM(block, BF),
                pltpu.VMEM((2, *block), BF),
                pltpu.SemaphoreType.DMA((rounds + 2,)),
                pltpu.SemaphoreType.DMA((rounds + 2,)),
            ],
            compiler_params=pltpu.CompilerParams(collective_id=0, has_side_effects=True),
        )(slab_green, coupling, left_lead_surface, sigma_right)

    in_specs = (
        P(None, ("energy", "slab"), None, None),
        P(None, ("energy", "slab"), None, None),
        P("energy", None, None),
        P("energy", None, None),
    )
    out_specs = P(None, ("energy", "slab"), None, None)
    return jax.shard_map(local, mesh=mesh, in_specs=in_specs, out_specs=out_specs, check_vma=False)
```

profile of v0, /device:TPU:17, one launch (start us, length us, event | category | flops | bytes accessed | tf_op | source)
XLA Modules:
  0.0 25.5 jit_solution(4924873770399165996)
XLA Ops:
  0.0 23.6 %shard_map.46 = f32[2,4,128,128]{3,2,1,0:T(8,128)} custom-call(bf16[2,4,128,128]{3,2,1,0:T(8,128)(2,1)} %green.1, bf16[2,4,128,128]{3,2,1,0:T(8,128)(2,1)} %link.1, bf16[2,128,128]{2,1,0:T(8,128)(2,1)} %lead.1, bf16[2,128,128]{2,1,0:T(8,128)(2,1)} %sigma.1), custom_call_target="tpu_custom_call" | custom-call | tf_op jit(solution)/shard_map/pallas_call | solution.py:237
  23.6 1.9 %copy.6 = f32[2,4,128,128]{3,2,1,0:T(8,128)} copy(f32[2,4,128,128]{3,2,1,0:T(8,128)} %shard_map.46) | data formatting | bytes 1048576
where the time goes:
time: 25.7 us; the launch traced here: 25.5 us
  Pallas kernels  23.6 us (92%)
  local copies, waits for them, and re-layouts  1.87 us (7%)
    pallas_call x1, Pallas kernels, local(): pl.pallas_call(functools.partial(kernel, rounds), out_shape=jax.ShapeDtyp...  23.6 us
    unnamed x1, local copies, waits for them, and re-layouts  1.87 us

commit v1 on v0

--- a/solution.py
+++ b/solution.py
@@ -94,7 +94,6 @@
     barrier = pltpu.get_barrier_semaphore()
     for other in [mate] + peers:
         pl.semaphore_signal(barrier, inc=1, device_id=(energy, other), device_id_type=MESH)
-    pl.semaphore_wait(barrier, rounds + 1)
 
     def remote(source, target, other, k):
         return pltpu.make_async_remote_copy(
@@ -112,40 +111,49 @@
     back = [product(c[i], g[i]) for i in range(layers)]
     hop = [halves(times_transpose(wide(back[i]), c[i])) for i in range(layers)]
 
-    m_up, s_up = [ahead[0]], [g[0]]
-    m_down, s_down = [back[-1]], [hop[-1]]
-    for i in range(1, layers):
-        s_up.append(plus(sandwich(ahead[i], s_up[-1]), g[i]))
-        m_up.append(product(ahead[i], m_up[-1]))
-        j = layers - 1 - i
-        s_down.insert(0, plus(sandwich(back[j], s_down[0]), hop[j]))
-        m_down.insert(0, product(back[j], m_down[0]))
-
-    put(own, m_up[-1], role, 0)
-    put(own, s_up[-1], role, 1)
-    put(own, m_down[0], 1 - role, 0)
-    put(own, s_down[0], 1 - role, 1)
+    def merged(first, second):
+        return (
+            product(second[0], first[0]),
+            plus(sandwich(second[0], first[1]), second[1]),
+        )
+
+    def whole(items):
+        while len(items) > 1:
+            rest = items[len(items) // 2 * 2 :]
+            items = [merged(*items[k : k + 2]) for k in range(0, len(items) - 1, 2)] + rest
+        return items[0]
+
+    up = [(ahead[i], g[i]) for i in range(layers)]
+    down = [(back[i], hop[i]) for i in reversed(range(layers))]
+    up_total, down_total = whole(up), whole(down)
+
+    put(own, up_total[0], role, 0)
+    put(own, up_total[1], role, 1)
+    put(own, down_total[0], 1 - role, 0)
+    put(own, down_total[1], 1 - role, 1)
+    pl.semaphore_wait(barrier, rounds + 1)
     copy = remote(own.at[1], pair, mate, 0)
     copy.start()
 
+    up_part, down_part = [up[0]], [down[0]]
+    for i in range(1, layers):
+        up_part.append(merged(up_part[-1], up[i]) if i + 1 < layers else up_total)
+        if i + 1 < layers:
+            down_part.append(merged(down_part[-1], down[i]))
     for i in range(layers):
-        put(factors, m_up[i], role, i)
+        m_part, s_part = up_part[i]
+        put(factors, m_part, role, i)
         if i + 1 < layers:
-            put(factors, product(g[i], m_down[i + 1]), 1 - role, i)
-            put(base, plus(s_up[i], sandwich(g[i], s_down[i + 1])), i)
+            m_rest, s_rest = down_part[layers - 2 - i]
+            put(factors, product(g[i], m_rest), 1 - role, i)
+            put(base, plus(s_part, sandwich(g[i], s_rest)), i)
         else:
             put(factors, g[i], 1 - role, i)
-            put(base, s_up[i], i)
+            put(base, s_part, i)
 
     copy.wait()
 
-    def merged(m_first, s_first, m_second, s_second):
-        return (
-            product(m_second, m_first),
-            plus(sandwich(m_second, s_first), s_second),
-        )
-
-    total = merged(get(own, 0, 0), get(own, 0, 1), get(pair, 0), get(pair, 1))
+    total = merged((get(own, 0, 0), get(own, 0, 1)), (get(pair, 0), get(pair, 1)))
     forward = role == 0
     start = (
         jnp.where(forward, lead[0], sigma[0]),
@@ -170,7 +178,7 @@
             m_before, s_before = pending()
         copy.wait()
         first, second = (get(board, r, 0, 0), get(board, r, 0, 1)), (get(board, r, 1, 0), get(board, r, 1, 1))
-        total = merged(*first, *second)
+        total = merged(first, second)
 
         def pending(r=r, first=first, m_old=m_before, s_old=s_before):
             if r == 0:
@@ -178,7 +186,7 @@
                     pick(sides[0], first[0], m_old),
                     pick(sides[0], (first[1][0].astype(F32), first[1][1].astype(F32)), s_old),
                 )
-            m_new, s_new = merged(*first, m_old, s_old)
+            m_new, s_new = merged(first, (m_old, s_old))
             return pick(sides[r], m_new, m_old), pick(sides[r], s_new, s_old)
 
     last = rounds - 1
@@ -251,7 +259,7 @@
                 pltpu.SemaphoreType.DMA((rounds + 2,)),
                 pltpu.SemaphoreType.DMA((rounds + 2,)),
             ],
-            compiler_params=pltpu.CompilerParams(collective_id=0, has_side_effects=True),
+            compiler_params=pltpu.CompilerParams(collective_id=0, has_side_effects=True, vmem_limit_bytes=16777216),
         )(slab_green, coupling, left_lead_surface, sigma_right)
 
     in_specs = (

time: 25.7 us -> 25.9 us (level)
  the two profiles are of different devices: /device:TPU:17 before, /device:TPU:0 now
where the time goes in v1:
time: 25.9 us; the launch traced here: 25.7 us
  Pallas kernels  21.3 us (82%)
  local copies, waits for them, and re-layouts  4.37 us (17%)
    pallas_call x1, Pallas kernels, local(): pl.pallas_call(functools.partial(kernel, rounds), out_shape=jax.ShapeDtyp...  21.3 us
    unnamed x9, local copies, waits for them, and re-layouts  4.37 us

profile of v1, /device:TPU:0, one launch (start us, length us, event | category | flops | bytes accessed | tf_op | source)
XLA Modules:
  0.0 25.7 jit_solution(10265931687659032168)
XLA Ops:
  0.0 0.0 copy-start
  0.0 0.9 %copy-done = bf16[2,4,128,128]{3,2,1,0:T(8,128)(2,1)S(1)} copy-done((bf16[2,4,128,128]{3,2,1,0:T(8,128)(2,1)S(1)}, bf16[2,4,128,128]{3,2,1,0:T(8,128)(2,1)}, u32[]{:S(2)}) %copy-start) | copy-done | bytes 262168
  1.0 0.0 copy-start.1
  1.0 0.9 %copy-done.1 = bf16[2,4,128,128]{3,2,1,0:T(8,128)(2,1)S(1)} copy-done((bf16[2,4,128,128]{3,2,1,0:T(8,128)(2,1)S(1)}, bf16[2,4,128,128]{3,2,1,0:T(8,128)(2,1)}, u32[]{:S(2)}) %copy-start.1) | copy-done | bytes 262168
  1.9 0.0 copy-start.2
  1.9 0.8 %copy-done.2 = bf16[2,128,128]{2,1,0:T(8,128)(2,1)S(1)} copy-done((bf16[2,128,128]{2,1,0:T(8,128)(2,1)S(1)}, bf16[2,128,128]{2,1,0:T(8,128)(2,1)}, u32[]{:S(2)}) %copy-start.2) | copy-done | bytes 65560
  2.7 0.0 copy-start.3
  2.7 0.8 %copy-done.3 = bf16[2,128,128]{2,1,0:T(8,128)(2,1)S(1)} copy-done((bf16[2,128,128]{2,1,0:T(8,128)(2,1)S(1)}, bf16[2,128,128]{2,1,0:T(8,128)(2,1)}, u32[]{:S(2)}) %copy-start.3) | copy-done | bytes 65560
  3.6 21.3 %shard_map.46 = f32[2,4,128,128]{3,2,1,0:T(8,128)S(1)} custom-call(bf16[2,4,128,128]{3,2,1,0:T(8,128)(2,1)S(1)} %copy-done, bf16[2,4,128,128]{3,2,1,0:T(8,128)(2,1)S(1)} %copy-done.1, bf16[2,128,128]{2,1,0:T(8,128)(2,1)S(1)} %copy-done.2, bf16[2,128,128]{2,1,0:T(8,128)(2,1)S(1)} %copy-done.3), custom_call_target="tpu_custom_call" | custom-call | tf_op jit(solution)/shard_map/pallas_call | solution.py:245
  24.9 0.8 %copy.6 = f32[2,4,128,128]{3,2,1,0:T(8,128)} copy(f32[2,4,128,128]{3,2,1,0:T(8,128)S(1)} %shard_map.46) | data formatting | bytes 1048576
Async XLA Ops:
  0.0 0.9 %copy-start = (bf16[2,4,128,128]{3,2,1,0:T(8,128)(2,1)S(1)}, bf16[2,4,128,128]{3,2,1,0:T(8,128)(2,1)}, u32[]{:S(2)}) copy-start(bf16[2,4,128,128]{3,2,1,0:T(8,128)(2,1)} %green.1) | copy-start | bytes 786436
  1.0 0.9 %copy-start.1 = (bf16[2,4,128,128]{3,2,1,0:T(8,128)(2,1)S(1)}, bf16[2,4,128,128]{3,2,1,0:T(8,128)(2,1)}, u32[]{:S(2)}) copy-start(bf16[2,4,128,128]{3,2,1,0:T(8,128)(2,1)} %link.1) | copy-start | bytes 786436
  1.9 0.8 %copy-start.2 = (bf16[2,128,128]{2,1,0:T(8,128)(2,1)S(1)}, bf16[2,128,128]{2,1,0:T(8,128)(2,1)}, u32[]{:S(2)}) copy-start(bf16[2,128,128]{2,1,0:T(8,128)(2,1)} %lead.1) | copy-start | bytes 196612
  2.7 0.8 %copy-start.3 = (bf16[2,128,128]{2,1,0:T(8,128)(2,1)S(1)}, bf16[2,128,128]{2,1,0:T(8,128)(2,1)}, u32[]{:S(2)}) copy-start(bf16[2,128,128]{2,1,0:T(8,128)(2,1)} %sigma.1) | copy-start | bytes 196612

commit v2 on v1

--- a/solution.py
+++ b/solution.py
@@ -67,11 +67,15 @@
 
 def kernel(
     rounds,
+    green_hbm,
+    link_hbm,
+    lead_hbm,
+    sigma_hbm,
+    out,
     green,
     link,
     lead,
     sigma,
-    out,
     own,
     pair,
     board,
@@ -82,7 +86,16 @@
     ends,
     send_sem,
     recv_sem,
+    load_sem,
 ):
+    loads = [
+        pltpu.make_async_copy(source, target, load_sem.at[k])
+        for k, (source, target) in enumerate(
+            [(green_hbm, green), (link_hbm, link), (lead_hbm, lead), (sigma_hbm, sigma)]
+        )
+    ]
+    for load in loads:
+        load.start()
     layers, width = green.shape[1], green.shape[2]
     energy, me = lax.axis_index("energy"), lax.axis_index("slab")
     role, chip = me % 2, me // 2
@@ -105,6 +118,8 @@
             device_id_type=MESH,
         )
 
+    for load in loads:
+        load.wait()
     g = [(green[0, i], green[1, i]) for i in range(layers)]
     c = [(link[0, i], link[1, i]) for i in range(layers)]
     ahead = [low(halves(times_transpose(wide(g[i]), c[i]))) for i in range(layers)]
@@ -245,9 +260,13 @@
         return pl.pallas_call(
             functools.partial(kernel, rounds),
             out_shape=jax.ShapeDtypeStruct(slab_green.shape, F32),
-            in_specs=[vmem] * 4,
+            in_specs=[pl.BlockSpec(memory_space=pltpu.HBM)] * 4,
             out_specs=vmem,
             scratch_shapes=[
+                pltpu.VMEM(slab_green.shape, BF),
+                pltpu.VMEM(coupling.shape, BF),
+                pltpu.VMEM(block, BF),
+                pltpu.VMEM(block, BF),
                 pltpu.VMEM((2, 2, *block), BF),
                 pltpu.VMEM((2, *block), BF),
                 pltpu.VMEM((max(rounds - 1, 1), 2, 2, *block), BF),
@@ -258,6 +277,7 @@
                 pltpu.VMEM((2, *block), BF),
                 pltpu.SemaphoreType.DMA((rounds + 2,)),
                 pltpu.SemaphoreType.DMA((rounds + 2,)),
+                pltpu.SemaphoreType.DMA((4,)),
             ],
             compiler_params=pltpu.CompilerParams(collective_id=0, has_side_effects=True, vmem_limit_bytes=16777216),
         )(slab_green, coupling, left_lead_surface, sigma_right)

time: 25.9 us -> 26.2 us (1.012)
  Pallas kernels: 21.3 us -> 21.6 us
    pallas_call x1, Pallas kernels: 21.3 us -> 21.6 us  [local(): pl.pallas_call(functools.partial(kernel, rounds), out_shape=jax.ShapeDtyp...]
where the time goes in v2:
time: 26.2 us; the launch traced here: 26 us
  Pallas kernels  21.6 us (82%)
  local copies, waits for them, and re-layouts  4.37 us (17%)
    pallas_call x1, Pallas kernels, local(): pl.pallas_call(functools.partial(kernel, rounds), out_shape=jax.ShapeDtyp...  21.6 us
    unnamed x9, local copies, waits for them, and re-layouts  4.37 us

profile of v2, /device:TPU:0, one launch (start us, length us, event | category | flops | bytes accessed | tf_op | source)
XLA Modules:
  0.0 26.0 jit_solution(13132728373866405773)
XLA Ops:
  0.0 0.0 copy-start
  0.0 0.9 %copy-done = bf16[2,4,128,128]{3,2,1,0:T(8,128)(2,1)S(1)} copy-done((bf16[2,4,128,128]{3,2,1,0:T(8,128)(2,1)S(1)}, bf16[2,4,128,128]{3,2,1,0:T(8,128)(2,1)}, u32[]{:S(2)}) %copy-start) | copy-done | bytes 262168
  1.0 0.0 copy-start.1
  1.0 0.9 %copy-done.1 = bf16[2,4,128,128]{3,2,1,0:T(8,128)(2,1)S(1)} copy-done((bf16[2,4,128,128]{3,2,1,0:T(8,128)(2,1)S(1)}, bf16[2,4,128,128]{3,2,1,0:T(8,128)(2,1)}, u32[]{:S(2)}) %copy-start.1) | copy-done | bytes 262168
  1.9 0.0 copy-start.2
  1.9 0.8 %copy-done.2 = bf16[2,128,128]{2,1,0:T(8,128)(2,1)S(1)} copy-done((bf16[2,128,128]{2,1,0:T(8,128)(2,1)S(1)}, bf16[2,128,128]{2,1,0:T(8,128)(2,1)}, u32[]{:S(2)}) %copy-start.2) | copy-done | bytes 65560
  2.7 0.0 copy-start.3
  2.7 0.8 %copy-done.3 = bf16[2,128,128]{2,1,0:T(8,128)(2,1)S(1)} copy-done((bf16[2,128,128]{2,1,0:T(8,128)(2,1)S(1)}, bf16[2,128,128]{2,1,0:T(8,128)(2,1)}, u32[]{:S(2)}) %copy-start.3) | copy-done | bytes 65560
  3.6 21.6 %shard_map.46 = f32[2,4,128,128]{3,2,1,0:T(8,128)S(1)} custom-call(bf16[2,4,128,128]{3,2,1,0:T(8,128)(2,1)S(1)} %copy-done, bf16[2,4,128,128]{3,2,1,0:T(8,128)(2,1)S(1)} %copy-done.1, bf16[2,128,128]{2,1,0:T(8,128)(2,1)S(1)} %copy-done.2, bf16[2,128,128]{2,1,0:T(8,128)(2,1)S(1)} %copy-done.3), custom_call_target="tpu_custom_call" | custom-call | tf_op jit(solution)/shard_map/pallas_call | solution.py:260
  25.2 0.8 %copy.6 = f32[2,4,128,128]{3,2,1,0:T(8,128)} copy(f32[2,4,128,128]{3,2,1,0:T(8,128)S(1)} %shard_map.46) | data formatting | bytes 1048576
Async XLA Ops:
  0.0 0.9 %copy-start = (bf16[2,4,128,128]{3,2,1,0:T(8,128)(2,1)S(1)}, bf16[2,4,128,128]{3,2,1,0:T(8,128)(2,1)}, u32[]{:S(2)}) copy-start(bf16[2,4,128,128]{3,2,1,0:T(8,128)(2,1)} %green_hbm.1) | copy-start | bytes 786436
  1.0 0.9 %copy-start.1 = (bf16[2,4,128,128]{3,2,1,0:T(8,128)(2,1)S(1)}, bf16[2,4,128,128]{3,2,1,0:T(8,128)(2,1)}, u32[]{:S(2)}) copy-start(bf16[2,4,128,128]{3,2,1,0:T(8,128)(2,1)} %link_hbm.1) | copy-start | bytes 786436
  1.9 0.8 %copy-start.2 = (bf16[2,128,128]{2,1,0:T(8,128)(2,1)S(1)}, bf16[2,128,128]{2,1,0:T(8,128)(2,1)}, u32[]{:S(2)}) copy-start(bf16[2,128,128]{2,1,0:T(8,128)(2,1)} %lead_hbm.1) | copy-start | bytes 196612
  2.7 0.8 %copy-start.3 = (bf16[2,128,128]{2,1,0:T(8,128)(2,1)S(1)}, bf16[2,128,128]{2,1,0:T(8,128)(2,1)}, u32[]{:S(2)}) copy-start(bf16[2,128,128]{2,1,0:T(8,128)(2,1)} %sigma_hbm.1) | copy-start | bytes 196612

commit v3 on v2

--- a/solution.py
+++ b/solution.py
@@ -280,7 +280,7 @@
                 pltpu.SemaphoreType.DMA((4,)),
             ],
             compiler_params=pltpu.CompilerParams(collective_id=0, has_side_effects=True, vmem_limit_bytes=16777216),
-        )(slab_green, coupling, left_lead_surface, sigma_right)
+        )(*[pltpu.with_memory_space_constraint(a, pltpu.HBM) for a in (slab_green, coupling, left_lead_surface, sigma_right)])
 
     in_specs = (
         P(None, ("energy", "slab"), None, None),

time: 26.2 us -> 23.2 us (0.89)
  local copies, waits for them, and re-layouts: 4.37 us -> 0.8 us
  Pallas kernels: 21.6 us -> 22.2 us
    unnamed x9 -> x1, local copies, waits for them, and re-layouts: 4.37 us -> 0.8 us
    pallas_call x1, Pallas kernels: 21.6 us -> 22.2 us  [local(): pl.pallas_call(functools.partial(kernel, rounds), out_shape=jax.ShapeDtyp...]
where the time goes in v3:
time: 23.2 us; the launch traced here: 23 us
  Pallas kernels  22.2 us (96%)
  local copies, waits for them, and re-layouts  0.8 us (3%)
    pallas_call x1, Pallas kernels, local(): pl.pallas_call(functools.partial(kernel, rounds), out_shape=jax.ShapeDtyp...  22.2 us
    unnamed x1, local copies, waits for them, and re-layouts  0.8 us

profile of v3, /device:TPU:0, one launch (start us, length us, event | category | flops | bytes accessed | tf_op | source)
XLA Modules:
  0.0 23.0 jit_solution(3368125687953088970)
XLA Ops:
  0.0 22.2 %shard_map.46 = f32[2,4,128,128]{3,2,1,0:T(8,128)S(1)} custom-call(bf16[2,4,128,128]{3,2,1,0:T(8,128)(2,1)} %green_hbm.1, bf16[2,4,128,128]{3,2,1,0:T(8,128)(2,1)} %link_hbm.1, bf16[2,128,128]{2,1,0:T(8,128)(2,1)} %lead_hbm.1, bf16[2,128,128]{2,1,0:T(8,128)(2,1)} %sigma_hbm.1), custom_call_target="tpu_custom_call" | custom-call | tf_op jit(solution)/shard_map/pallas_call | solution.py:260
  22.3 0.8 %copy.6 = f32[2,4,128,128]{3,2,1,0:T(8,128)} copy(f32[2,4,128,128]{3,2,1,0:T(8,128)S(1)} %shard_map.46) | data formatting | bytes 1048576

commit v4 on v3

--- a/solution.py
+++ b/solution.py
@@ -81,8 +81,8 @@
     board,
     factors,
     base,
-    enter,
-    onward,
+    inbox,
+    outbox,
     ends,
     send_sem,
     recv_sem,
@@ -100,23 +100,58 @@
     energy, me = lax.axis_index("energy"), lax.axis_index("slab")
     role, chip = me % 2, me // 2
     mate = me + 1 - 2 * role
-    bits = [(chip // 2**r) % 2 for r in range(rounds)]
-    peers = [me + (1 - 2 * bits[r]) * 2 ** (r + 1) for r in range(rounds)]
-    sides = [(bits[r] + role) % 2 for r in range(rounds)]
+    bit = chip % 2
+    side = (bit + role) % 2
+    pal = me + (1 - 2 * bit) * 2
+    steps = rounds - 1
+    spot = chip // 2
+    place = spot + role * (2**steps - 1 - 2 * spot)
+    stride = (1 - 2 * role) * 4
+    lows = [place // 2 ** (k + 1) * 2 ** (k + 1) for k in range(steps)]
+    gives = [place == lows[k] + 2**k - 1 for k in range(steps)]
+    takes = [(place // 2**k) % 2 == 1 for k in range(steps)]
+    givers = [me + stride * (lows[k] + 2**k - 1 - place) for k in range(steps)]
 
     barrier = pltpu.get_barrier_semaphore()
-    for other in [mate] + peers:
+
+    def greet(other):
         pl.semaphore_signal(barrier, inc=1, device_id=(energy, other), device_id_type=MESH)
 
-    def remote(source, target, other, k):
+    expected = 2
+    greet(mate)
+    greet(pal)
+    for k in range(steps):
+        expected = expected + jnp.where(gives[k], 2**k, 0) + jnp.where(takes[k], 1, 0)
+
+        @pl.when(gives[k])
+        def _():
+            for d in range(2**k):
+                greet(me + stride * (1 + d))
+
+        @pl.when(takes[k])
+        def _():
+            greet(givers[k])
+
+    def remote(source, target, other, sender, receiver):
         return pltpu.make_async_remote_copy(
             src_ref=source,
             dst_ref=target,
-            send_sem=send_sem.at[k],
-            recv_sem=recv_sem.at[k],
+            send_sem=send_sem.at[sender],
+            recv_sem=recv_sem.at[receiver],
             device_id=(energy, other),
             device_id_type=MESH,
         )
+
+    zeros = jnp.zeros((width, width), BF)
+    for k in range(steps):
+
+        @pl.when(jnp.logical_not(takes[k]))
+        def _():
+            put(inbox, (zeros, zeros), k, 1)
+
+        @pl.when(jnp.logical_or(jnp.logical_not(takes[k]), lows[k] == 0))
+        def _():
+            put(inbox, (zeros, zeros), k, 0)
 
     for load in loads:
         load.wait()
@@ -146,9 +181,9 @@
     put(own, up_total[1], role, 1)
     put(own, down_total[0], 1 - role, 0)
     put(own, down_total[1], 1 - role, 1)
-    pl.semaphore_wait(barrier, rounds + 1)
-    copy = remote(own.at[1], pair, mate, 0)
-    copy.start()
+    pl.semaphore_wait(barrier, expected)
+    swap = remote(own.at[1], pair, mate, 0, 0)
+    swap.start()
 
     up_part, down_part = [up[0]], [down[0]]
     for i in range(1, layers):
@@ -166,8 +201,7 @@
             put(factors, g[i], 1 - role, i)
             put(base, s_part, i)
 
-    copy.wait()
-
+    swap.wait_recv()
     total = merged((get(own, 0, 0), get(own, 0, 1)), (get(pair, 0), get(pair, 1)))
     forward = role == 0
     start = (
@@ -176,54 +210,108 @@
     )
     row = lax.broadcasted_iota(jnp.int32, (width, width), 0)
     column = lax.broadcasted_iota(jnp.int32, (width, width), 1)
-    square = jnp.where(row == column, 1.0, 0.0).astype(F32)
-    nothing = jnp.zeros((width, width), F32)
-    m_before, s_before = (square.astype(BF), nothing.astype(BF)), (nothing, nothing)
-
-    def pick(side, a, b):
-        return jnp.where(side == 1, a[0], b[0]), jnp.where(side == 1, a[1], b[1])
-
-    pending = None
-    for r in range(rounds - 1):
-        put(board, total[0], r, sides[r], 0)
-        put(board, total[1], r, sides[r], 1)
-        copy = remote(board.at[r, sides[r]], board.at[r, sides[r]], peers[r], 1 + r)
-        copy.start()
-        if pending is not None:
-            m_before, s_before = pending()
-        copy.wait()
-        first, second = (get(board, r, 0, 0), get(board, r, 0, 1)), (get(board, r, 1, 0), get(board, r, 1, 1))
-        total = merged(first, second)
-
-        def pending(r=r, first=first, m_old=m_before, s_old=s_before):
-            if r == 0:
-                return (
-                    pick(sides[0], first[0], m_old),
-                    pick(sides[0], (first[1][0].astype(F32), first[1][1].astype(F32)), s_old),
+    square = jnp.where(row == column, 1.0, 0.0).astype(BF)
+
+    def wider(value):
+        return value[0].astype(F32), value[1].astype(F32)
+
+    def pick(test, a, b):
+        return jnp.where(test, a[0], b[0]), jnp.where(test, a[1], b[1])
+
+    def choose(test, a, b):
+        return pick(test, a[0], b[0]), pick(test, a[1], b[1])
+
+    put(board, total[0], side, 0)
+    put(board, total[1], side, 1)
+    cross = remote(board.at[side], board.at[side], pal, 1, 1)
+    cross.start()
+    cross.wait_recv()
+    first = (get(board, 0, 0), wider(get(board, 0, 1)))
+    second = (get(board, 1, 0), wider(get(board, 1, 1)))
+    total = merged(first, second)
+    none = (zeros, zeros)
+    head = place == 0
+
+    def settled(value):
+        return pick(head, none, value[0]), pick(
+            head, plus(sandwich(value[0], start), value[1]), value[1]
+        )
+
+    total = settled(total)
+
+    def deliveries(k):
+        found = []
+        for d in range(2**k):
+            other = me + stride * (1 + d)
+            at = 2 + 2 * (2**k - 1 + d)
+            found.append(
+                (
+                    remote(outbox.at[k, 1], inbox.at[k, 1], other, at, 2 + 2 * k),
+                    remote(outbox.at[k, 0], inbox.at[k, 0], other, at + 1, 3 + 2 * k),
                 )
-            m_new, s_new = merged(first, (m_old, s_old))
-            return pick(sides[r], m_new, m_old), pick(sides[r], s_new, s_old)
-
-    last = rounds - 1
-    put(onward, plus(sandwich(total[0], start), total[1]))
-    copy = remote(onward, enter, peers[last], rounds)
-
-    @pl.when(sides[last] == 0)
-    def _():
-        copy.start()
-        put(enter, start)
-
-    if pending is not None:
-        m_before, s_before = pending()
-
-    @pl.when(sides[last] == 1)
-    def _():
-        copy.wait_recv()
-
-    entering = plus(sandwich(m_before, get(enter)), s_before)
+            )
+        return found
+
+    def send(k):
+        @pl.when(gives[k])
+        def _():
+            put(outbox, total[1], k, 1)
+            put(outbox, total[0], k, 0)
+            sent = deliveries(k)
+            for constant, _ in sent:
+                constant.start()
+            if k + 1 < steps:
+
+                @pl.when(lows[k] != 0)
+                def _():
+                    for _, linear in sent:
+                        linear.start()
+
+    def receive(k):
+        @pl.when(takes[k])
+        def _():
+            constant, linear = deliveries(k)[0]
+            constant.wait_recv()
+            if k + 1 < steps:
+
+                @pl.when(lows[k] != 0)
+                def _():
+                    linear.wait_recv()
+
+        return get(inbox, k, 0), wider(get(inbox, k, 1))
+
+    def finish(k):
+        @pl.when(gives[k])
+        def _():
+            sent = deliveries(k)
+            for constant, _ in sent:
+                constant.wait_send()
+            if k + 1 < steps:
+
+                @pl.when(lows[k] != 0)
+                def _():
+                    for _, linear in sent:
+                        linear.wait_send()
+
+    if steps:
+        send(0)
+    before = settled(
+        (
+            pick(side == 1, first[0], (square, zeros)),
+            pick(side == 1, first[1], wider(none)),
+        )
+    )
+    for k in range(steps):
+        got = receive(k)
+        if k + 1 < steps:
+            total = choose(takes[k], merged(got, total), total)
+            send(k + 1)
+        before = choose(takes[k], merged(got, before), before)
+    entering = before[1]
     put(ends, entering, role)
     put(pair, plus(sandwich(get(own, 0, 0), entering), get(own, 0, 1)), 0)
-    share = remote(pair.at[0], ends.at[role], mate, rounds + 1)
+    last = 2 + 2 * steps
+    share = remote(pair.at[0], ends.at[role], mate, 2 * 2**steps, last)
     share.start()
 
     def spread(k, middle):
@@ -237,16 +325,18 @@
     mine = spread(0, entering)
     for i in range(layers):
         put(base, plus(get(base, i), mine[i]), i)
-    share.wait()
+    share.wait_recv()
     theirs = spread(1, get(ends, 1 - role))
     for i in range(layers):
         value = plus(get(base, i), theirs[i])
         out[0, i] = value[0]
         out[1, i] = value[1]
 
-    @pl.when(sides[last] == 0)
-    def _():
-        copy.wait_send()
+    swap.wait_send()
+    cross.wait_send()
+    share.wait_send()
+    for k in range(steps):
+        finish(k)
 
 
 def solution(mesh):
@@ -269,14 +359,14 @@
                 pltpu.VMEM(block, BF),
                 pltpu.VMEM((2, 2, *block), BF),
                 pltpu.VMEM((2, *block), BF),
-                pltpu.VMEM((max(rounds - 1, 1), 2, 2, *block), BF),
+                pltpu.VMEM((2, 2, *block), BF),
                 pltpu.VMEM((2, layers, *block), BF),
                 pltpu.VMEM((layers, *block), F32),
-                pltpu.VMEM(block, BF),
-                pltpu.VMEM(block, BF),
+                pltpu.VMEM((max(rounds - 1, 1), 2, *block), BF),
+                pltpu.VMEM((max(rounds - 1, 1), 2, *block), BF),
                 pltpu.VMEM((2, *block), BF),
-                pltpu.SemaphoreType.DMA((rounds + 2,)),
-                pltpu.SemaphoreType.DMA((rounds + 2,)),
+                pltpu.SemaphoreType.DMA((2**rounds + 1,)),
+                pltpu.SemaphoreType.DMA((2 * rounds + 1,)),
                 pltpu.SemaphoreType.DMA((4,)),
             ],
             compiler_params=pltpu.CompilerParams(collective_id=0, has_side_effects=True, vmem_limit_bytes=16777216),

time: 23.2 us -> 22.2 us (0.957)
  Pallas kernels: 22.2 us -> 21.3 us
    pallas_call x1, Pallas kernels: 22.2 us -> 21.3 us  [local(): pl.pallas_call(functools.partial(kernel, rounds), out_shape=jax.ShapeDtyp...]
where the time goes in v4:
time: 22.2 us; the launch traced here: 22.1 us
  Pallas kernels  21.3 us (96%)
  local copies, waits for them, and re-layouts  0.8 us (4%)
    pallas_call x1, Pallas kernels, local(): pl.pallas_call(functools.partial(kernel, rounds), out_shape=jax.ShapeDtyp...  21.3 us
    unnamed x1, local copies, waits for them, and re-layouts  0.8 us

profile of v4, /device:TPU:0, one launch (start us, length us, event | category | flops | bytes accessed | tf_op | source)
XLA Modules:
  0.0 22.1 jit_solution(5785685722308888078)
XLA Ops:
  0.0 21.3 %shard_map.46 = f32[2,4,128,128]{3,2,1,0:T(8,128)S(1)} custom-call(bf16[2,4,128,128]{3,2,1,0:T(8,128)(2,1)} %green_hbm.1, bf16[2,4,128,128]{3,2,1,0:T(8,128)(2,1)} %link_hbm.1, bf16[2,128,128]{2,1,0:T(8,128)(2,1)} %lead_hbm.1, bf16[2,128,128]{2,1,0:T(8,128)(2,1)} %sigma_hbm.1), custom_call_target="tpu_custom_call" | custom-call | tf_op jit(solution)/shard_map/pallas_call | solution.py:350
  21.3 0.8 %copy.6 = f32[2,4,128,128]{3,2,1,0:T(8,128)} copy(f32[2,4,128,128]{3,2,1,0:T(8,128)S(1)} %shard_map.46) | data formatting | bytes 1048576

commit v5 on v4

--- a/solution.py
+++ b/solution.py
@@ -78,6 +78,7 @@
     sigma,
     own,
     pair,
+    given,
     board,
     factors,
     base,
@@ -202,6 +203,9 @@
             put(base, s_part, i)
 
     swap.wait_recv()
+    last = 2 + 2 * steps
+    hint = remote(own.at[0], given, mate, 2 * 2**steps + 1, last + 1)
+    hint.start()
     total = merged((get(own, 0, 0), get(own, 0, 1)), (get(pair, 0), get(pair, 1)))
     forward = role == 0
     start = (
@@ -301,6 +305,11 @@
             pick(side == 1, first[1], wider(none)),
         )
     )
+    hint.wait_recv()
+    for i in range(layers):
+        factor = get(factors, 1, i)
+        put(base, plus(get(base, i), sandwich(factor, get(given, 1))), i)
+        put(factors, product(factor, get(given, 0)), 1, i)
     for k in range(steps):
         got = receive(k)
         if k + 1 < steps:
@@ -309,9 +318,7 @@
         before = choose(takes[k], merged(got, before), before)
     entering = before[1]
     put(ends, entering, role)
-    put(pair, plus(sandwich(get(own, 0, 0), entering), get(own, 0, 1)), 0)
-    last = 2 + 2 * steps
-    share = remote(pair.at[0], ends.at[role], mate, 2 * 2**steps, last)
+    share = remote(ends.at[role], ends.at[role], mate, 2 * 2**steps, last)
     share.start()
 
     def spread(k, middle):
@@ -333,6 +340,7 @@
         out[1, i] = value[1]
 
     swap.wait_send()
+    hint.wait_send()
     cross.wait_send()
     share.wait_send()
     for k in range(steps):
@@ -359,14 +367,15 @@
                 pltpu.VMEM(block, BF),
                 pltpu.VMEM((2, 2, *block), BF),
                 pltpu.VMEM((2, *block), BF),
+                pltpu.VMEM((2, *block), BF),
                 pltpu.VMEM((2, 2, *block), BF),
                 pltpu.VMEM((2, layers, *block), BF),
                 pltpu.VMEM((layers, *block), F32),
                 pltpu.VMEM((max(rounds - 1, 1), 2, *block), BF),
                 pltpu.VMEM((max(rounds - 1, 1), 2, *block), BF),
                 pltpu.VMEM((2, *block), BF),
-                pltpu.SemaphoreType.DMA((2**rounds + 1,)),
-                pltpu.SemaphoreType.DMA((2 * rounds + 1,)),
+                pltpu.SemaphoreType.DMA((2**rounds + 2,)),
+                pltpu.SemaphoreType.DMA((2 * rounds + 2,)),
                 pltpu.SemaphoreType.DMA((4,)),
             ],
             compiler_params=pltpu.CompilerParams(collective_id=0, has_side_effects=True, vmem_limit_bytes=16777216),

time: 22.2 us -> 21.9 us (0.986)
  Pallas kernels: 21.3 us -> 20.9 us
    pallas_call x1, Pallas kernels: 21.3 us -> 20.9 us  [local(): pl.pallas_call(functools.partial(kernel, rounds), out_shape=jax.ShapeDtyp...]
where the time goes in v5:
time: 21.9 us; the launch traced here: 21.8 us
  Pallas kernels  20.9 us (95%)
  local copies, waits for them, and re-layouts  0.8 us (4%)
    pallas_call x1, Pallas kernels, local(): pl.pallas_call(functools.partial(kernel, rounds), out_shape=jax.ShapeDtyp...  20.9 us
    unnamed x1, local copies, waits for them, and re-layouts  0.8 us

profile of v5, /device:TPU:0, one launch (start us, length us, event | category | flops | bytes accessed | tf_op | source)
XLA Modules:
  0.0 21.8 jit_solution(8280220064680807182)
XLA Ops:
  0.0 20.9 %shard_map.46 = f32[2,4,128,128]{3,2,1,0:T(8,128)S(1)} custom-call(bf16[2,4,128,128]{3,2,1,0:T(8,128)(2,1)} %green_hbm.1, bf16[2,4,128,128]{3,2,1,0:T(8,128)(2,1)} %link_hbm.1, bf16[2,128,128]{2,1,0:T(8,128)(2,1)} %lead_hbm.1, bf16[2,128,128]{2,1,0:T(8,128)(2,1)} %sigma_hbm.1), custom_call_target="tpu_custom_call" | custom-call | tf_op jit(solution)/shard_map/pallas_call | solution.py:358
  21.0 0.8 %copy.6 = f32[2,4,128,128]{3,2,1,0:T(8,128)} copy(f32[2,4,128,128]{3,2,1,0:T(8,128)S(1)} %shard_map.46) | data formatting | bytes 1048576

commit v6 on v5

--- a/solution.py
+++ b/solution.py
@@ -305,12 +305,22 @@
             pick(side == 1, first[1], wider(none)),
         )
     )
-    hint.wait_recv()
-    for i in range(layers):
-        factor = get(factors, 1, i)
-        put(base, plus(get(base, i), sandwich(factor, get(given, 1))), i)
-        put(factors, product(factor, get(given, 0)), 1, i)
+    def fold():
+        hint.wait_recv()
+        parts = [get(factors, 1, i) for i in range(layers)]
+        rows = jnp.concatenate([wide(part) for part in parts], axis=0)
+        linear = times(rows, get(given, 0))
+        inner = times(rows, get(given, 1)).astype(BF)
+        for i in range(layers):
+            cut = slice(i * width, (i + 1) * width)
+            put(base, plus(get(base, i), halves(times_transpose(inner[cut], parts[i]))), i)
+            put(factors, halves(linear[cut]), 1, i)
+
+    if not steps:
+        fold()
     for k in range(steps):
+        if k + 1 == steps:
+            fold()
         got = receive(k)
         if k + 1 < steps:
             total = choose(takes[k], merged(got, total), total)

time: 21.9 us -> 21.9 us (level)
  no operation moved by 1% of the time
where the time goes in v6:
time: 21.9 us; the launch traced here: 21.8 us
  Pallas kernels  21 us (96%)
  local copies, waits for them, and re-layouts  0.8 us (4%)
    pallas_call x1, Pallas kernels, local(): pl.pallas_call(functools.partial(kernel, rounds), out_shape=jax.ShapeDtyp...  21 us
    unnamed x1, local copies, waits for them, and re-layouts  0.8 us

profile of v6, /device:TPU:0, one launch (start us, length us, event | category | flops | bytes accessed | tf_op | source)
XLA Modules:
  0.0 21.8 jit_solution(6354472374450013358)
XLA Ops:
  0.0 21.0 %shard_map.46 = f32[2,4,128,128]{3,2,1,0:T(8,128)S(1)} custom-call(bf16[2,4,128,128]{3,2,1,0:T(8,128)(2,1)} %green_hbm.1, bf16[2,4,128,128]{3,2,1,0:T(8,128)(2,1)} %link_hbm.1, bf16[2,128,128]{2,1,0:T(8,128)(2,1)} %lead_hbm.1, bf16[2,128,128]{2,1,0:T(8,128)(2,1)} %sigma_hbm.1), custom_call_target="tpu_custom_call" | custom-call | tf_op jit(solution)/shard_map/pallas_call | solution.py:368
  21.0 0.8 %copy.6 = f32[2,4,128,128]{3,2,1,0:T(8,128)} copy(f32[2,4,128,128]{3,2,1,0:T(8,128)S(1)} %shard_map.46) | data formatting | bytes 1048576

commit v7 on v5

--- a/solution.py
+++ b/solution.py
@@ -154,7 +154,7 @@
         def _():
             put(inbox, (zeros, zeros), k, 0)
 
-    for load in loads:
+    for load in loads[:2]:
         load.wait()
     g = [(green[0, i], green[1, i]) for i in range(layers)]
     c = [(link[0, i], link[1, i]) for i in range(layers)]
@@ -202,6 +202,8 @@
             put(factors, g[i], 1 - role, i)
             put(base, s_part, i)
 
+    for load in loads[2:]:
+        load.wait()
     swap.wait_recv()
     last = 2 + 2 * steps
     hint = remote(own.at[0], given, mate, 2 * 2**steps + 1, last + 1)
@@ -262,7 +264,7 @@
             put(outbox, total[1], k, 1)
             put(outbox, total[0], k, 0)
             sent = deliveries(k)
-            for constant, _ in sent:
+            for constant, _ in reversed(sent):
                 constant.start()
             if k + 1 < steps:
 

time: 21.9 us -> 21.2 us (0.968)
  Pallas kernels: 20.9 us -> 20.2 us
    pallas_call x1, Pallas kernels: 20.9 us -> 20.2 us  [local(): pl.pallas_call(functools.partial(kernel, rounds), out_shape=jax.ShapeDtyp...]
where the time goes in v7:
time: 21.2 us; the launch traced here: 21 us
  Pallas kernels  20.2 us (95%)
  local copies, waits for them, and re-layouts  0.8 us (4%)
    pallas_call x1, Pallas kernels, local(): pl.pallas_call(functools.partial(kernel, rounds), out_shape=jax.ShapeDtyp...  20.2 us
    unnamed x1, local copies, waits for them, and re-layouts  0.8 us

profile of v7, /device:TPU:0, one launch (start us, length us, event | category | flops | bytes accessed | tf_op | source)
XLA Modules:
  0.0 21.0 jit_solution(1801112721195671466)
XLA Ops:
  0.0 20.2 %shard_map.46 = f32[2,4,128,128]{3,2,1,0:T(8,128)S(1)} custom-call(bf16[2,4,128,128]{3,2,1,0:T(8,128)(2,1)} %green_hbm.1, bf16[2,4,128,128]{3,2,1,0:T(8,128)(2,1)} %link_hbm.1, bf16[2,128,128]{2,1,0:T(8,128)(2,1)} %lead_hbm.1, bf16[2,128,128]{2,1,0:T(8,128)(2,1)} %sigma_hbm.1), custom_call_target="tpu_custom_call" | custom-call | tf_op jit(solution)/shard_map/pallas_call | solution.py:360
  20.2 0.8 %copy.6 = f32[2,4,128,128]{3,2,1,0:T(8,128)} copy(f32[2,4,128,128]{3,2,1,0:T(8,128)S(1)} %shard_map.46) | data formatting | bytes 1048576
